TPU v7x, 32 devices: a whole 2x2x4 slice. The times are simulated.
32 devices in a mesh: group: 2 (over y), ctx: 16 (over z, x, core).
Axes of the slice: x: 2, y: 2, z: 4, core: 2. Of those that a mesh axis runs over, the one named last changes fastest.
Arguments:
- queries: bfloat16 [4096, 2048], P(('group', 'ctx')), parts along dimension 0, may hold values from -28 to 28
- fresh_kv: bfloat16 [4096, 512], P(('group', 'ctx')), parts along dimension 0, may hold values from -10 to 10
- kv_cache: bfloat16 [256, 128, 512], P(('group', 'ctx')), parts along dimension 0, may hold values from -8 to 8
- selection: int32 [32, 2], P('group'), parts along dimension 0, may hold values from 0 to 127, as said below
- ctx_lengths: int32 [4], P('group'), parts along dimension 0, may hold values from 4096 to 8192, as said below
- residual_rows: bfloat16 [2048, 2048], P(('group', 'ctx')), parts along dimension 0, may hold values from -400 to 400
- norm_gain: float32 [2048], replicated, may hold values from 0.1 to 1.9
- w_gate_up: bfloat16 [16, 2048, 1536], P('ctx'), may hold values from -0.125 to 0.125
- w_down: bfloat16 [16, 768, 2048], P('ctx'), may hold values from -0.21875 to 0.21875
- expert_ids: int32 [2048, 8], P(('group', 'ctx')), parts along dimension 0, may hold values from 0 to 15, all different within a row; in each aligned block of 64 rows (0 to 63, 64 to 127, ...) at most 40 rows name the same one
- gate_weights: float32 [2048, 8], P(('group', 'ctx')), parts along dimension 0, may hold values from 0.1 to 0.4
Outputs:
- attention: bfloat16 [4096, 2048], P(('group', 'ctx')), parts along dimension 0
- expert_out: bfloat16 [2048, 2048], P(('group', 'ctx')), parts along dimension 0
There are 2 independent parts, one for each index of `group`. A program takes and returns all parts, laid end to end along the dimension named above; an argument that names none is the same for every part. Nothing has to cross between parts.
Inputs may be any that keep to these rules, and one draw needn't show every extreme that they name: `selection`: row r names the 2 cache blocks read by the query block of device r: blocks b of request q = r // 8, that is b mod 2 = q, with (b // 2) * 128 < ctx_lengths[q]; no two of them are held by the same device. `ctx_lengths`: entry q counts the cached tokens of request q; one of the two entries is 8192. `expert_ids`: each row names 8 different experts; the 64 tokens of one device name one expert at most 40 times, a bound that some block reaches.
All inputs are finite; a program needn't handle non-finite values.
Results may differ from a plain program's by a relative error of at most 0.007.
Values may be sent and summed in bfloat16 or wider, within the bound.
A program may use at most 128 MiB of HBM per device.

v0:
```python
import jax
import jax.numpy as jnp
from jax import lax
from jax.sharding import PartitionSpec as P

HEADS = 16
KV_HEADS = 2
HEAD_DIM = 128
TOPK = 8
BLOCK = 128


masked_score = -1e30
epsilon = 1e-06


def rms_normed(hidden_rows, gain_row):
    values = hidden_rows.astype(jnp.float32)
    mean_square = jnp.mean(values * values, axis=-1, keepdims=True)
    return (values * lax.rsqrt(mean_square + epsilon) * gain_row).astype(jnp.bfloat16)


def key_usable(chosen, ctx_lengths):
    request = chosen % 2
    within = chosen // 2
    limits = jnp.take(ctx_lengths, request)
    position = within[:, None] * BLOCK + jnp.arange(BLOCK, dtype=jnp.int32)[None, :]
    return (position < limits[:, None]).reshape(-1)


def head_scores(queried, kv_rows, usable_mask, kv_head):
    offset = kv_head * HEAD_DIM
    key_part = kv_rows[:, offset : offset + HEAD_DIM]
    value_start = (KV_HEADS + kv_head) * HEAD_DIM
    value_part = kv_rows[:, value_start : value_start + HEAD_DIM]
    scores = jnp.einsum(
        "tgd,ld->gtl", queried[:, kv_head], key_part, preferred_element_type=jnp.float32
    ) * HEAD_DIM ** (-0.5)
    return (jnp.where(usable_mask[None], scores, masked_score), value_part)


def attend_rows(queried, kv_rows, usable_mask):
    pieces_out = []
    for kv_head in range(KV_HEADS):
        scores, value_part = head_scores(queried, kv_rows, usable_mask, kv_head)
        largest = jnp.max(scores, axis=-1, keepdims=True)
        weights = jnp.exp(scores - largest)
        totals = jnp.sum(weights, axis=-1)
        blended = jnp.einsum(
            "gtl,ld->tgd",
            weights.astype(jnp.bfloat16),
            value_part,
            preferred_element_type=jnp.float32,
        )
        pieces_out.append(blended / jnp.transpose(totals)[:, :, None])
    return jnp.stack(pieces_out, axis=1)


def attention_layer(queries, fresh_kv, kv_cache, selection, ctx_lengths):
    device_index = lax.axis_index("ctx")
    stored = kv_cache.shape[0]
    tokens = queries.shape[0]
    groups = HEADS // KV_HEADS
    queried = queries.reshape(tokens, KV_HEADS, groups, HEAD_DIM)
    chosen_blocks = lax.dynamic_index_in_dim(selection, device_index, 0, keepdims=False)
    causal = jnp.arange(tokens)[:, None] >= jnp.arange(tokens)[None, :]
    wanted = selection // stored == device_index
    local_index = jnp.sum(jnp.where(wanted, selection % stored, 0), axis=1)
    asked = jnp.any(wanted, axis=1)
    outgoing = jnp.where(asked[:, None, None], jnp.take(kv_cache, local_index, axis=0), 0)
    arrived = lax.all_to_all(outgoing, "ctx", split_axis=0, concat_axis=0, tiled=True)
    blocks = jnp.take(arrived, chosen_blocks // stored, axis=0)
    kv_rows = jnp.concatenate([blocks.reshape(-1, blocks.shape[2]), fresh_kv], axis=0)
    usable = key_usable(chosen_blocks, ctx_lengths)
    usable_mask = jnp.concatenate(
        [jnp.broadcast_to(usable[None, :], (tokens, usable.shape[0])), causal], axis=1
    )
    blended = attend_rows(queried, kv_rows, usable_mask)
    return blended.reshape(tokens, HEADS * HEAD_DIM).astype(jnp.bfloat16)


def slot_places(expert_ids, experts, capacity):
    flat_ids = expert_ids.reshape(-1)
    one_hot = (flat_ids[:, None] == jnp.arange(experts, dtype=jnp.int32)[None, :]).astype(jnp.int32)
    earlier = jnp.cumsum(one_hot, axis=0) - one_hot
    slot_rank = jnp.sum(earlier * one_hot, axis=1)
    placement = flat_ids * capacity + slot_rank
    amount = expert_ids.shape[0] * expert_ids.shape[1]
    owner_token = jnp.arange(amount, dtype=jnp.int32) // expert_ids.shape[1]
    token_table = jnp.zeros((experts * capacity,), jnp.int32).at[placement].set(owner_token)
    filled = jnp.zeros((experts * capacity,), jnp.int32).at[placement].set(1)
    return (placement, token_table, filled)


def expert_rows(token_rows, gate_up, down_proj):
    gate_and_up = jnp.dot(token_rows, gate_up, preferred_element_type=jnp.float32)
    hidden_units = down_proj.shape[0]
    active = (jax.nn.silu(gate_and_up[:, :hidden_units]) * gate_and_up[:, hidden_units:]).astype(
        jnp.bfloat16
    )
    return jnp.dot(active, down_proj, preferred_element_type=jnp.float32).astype(jnp.bfloat16)


def expert_layer(residual_rows, norm_gain, w_gate_up, w_down, expert_ids, gate_weights):
    experts = lax.axis_size("ctx")
    capacity = max(3, 5 * expert_ids.shape[0] * TOPK // (4 * experts))
    normed = rms_normed(residual_rows, norm_gain)
    placement, token_table, filled = slot_places(expert_ids, experts, capacity)
    outgoing = jnp.where(filled[:, None] > 0, jnp.take(normed, token_table, axis=0), 0)
    outgoing = outgoing.reshape(experts, capacity, normed.shape[1])
    arrived = lax.all_to_all(outgoing, "ctx", split_axis=0, concat_axis=0, tiled=True)
    amount = arrived.shape[1]
    produced = expert_rows(arrived.reshape(-1, arrived.shape[2]), w_gate_up[0], w_down[0])
    returned = lax.all_to_all(
        produced.reshape(experts, amount, produced.shape[1]),
        "ctx",
        split_axis=0,
        concat_axis=0,
        tiled=True,
    )
    picked = jnp.take(
        returned.reshape(experts * capacity, returned.shape[2]), placement, axis=0
    ).astype(jnp.float32)
    picked = picked * gate_weights.reshape(-1)[:, None]
    summed = jnp.sum(
        picked.reshape(expert_ids.shape[0], expert_ids.shape[1], picked.shape[1]), axis=1
    )
    return summed.astype(jnp.bfloat16)


def shards(
    queries,
    fresh_kv,
    kv_cache,
    selection,
    ctx_lengths,
    residual_rows,
    norm_gain,
    w_gate_up,
    w_down,
    expert_ids,
    gate_weights,
):
    attention = attention_layer(queries, fresh_kv, kv_cache, selection, ctx_lengths)
    expert_out = expert_layer(residual_rows, norm_gain, w_gate_up, w_down, expert_ids, gate_weights)
    return (attention, expert_out)


def solution(mesh):
    return jax.shard_map(
        shards,
        mesh=mesh,
        in_specs=(
            P(("group", "ctx"), None),
            P(("group", "ctx"), None),
            P(("group", "ctx"), None, None),
            P("group", None),
            P("group"),
            P(("group", "ctx"), None),
            P(),
            P("ctx", None, None),
            P("ctx", None, None),
            P(("group", "ctx"), None),
            P(("group", "ctx"), None),
        ),
        out_specs=(P(("group", "ctx"), None), P(("group", "ctx"), None)),
        check_vma=False,
    )
```

profile of v0, /device:TPU:11, one launch (start us, length us, event | category | flops | bytes accessed | tf_op | source)
XLA Modules:
  0.0 212.5 jit_solution(11185858738945084503)
XLA Ops:
  0.6 0.9 copy.40
  1.6 0.1 eq.38
  1.7 0.1 reshape.338
  1.7 0.7 broadcast_multiply_fusion
  2.5 1.2 reduce-window.6
  3.6 0.2 slice_reduce_fusion
  3.9 0.1 copy.45
  3.9 0.1 mul.85
  4.0 0.1 fusion.37
  4.2 2.4 %scatter_custom_fusion.1 = s32[640]{0:T(1024)S(1)} fusion(s32[512]{0:T(512)S(1)} %bitcast.127, s32[512]{0:T(512)S(1)} %add_select_fusion, s32[]{:T(128)} %constant.153.clone.1), kind=kCustom, calls=%fused_computation.93 | custom fusion | bytes 2564 | tf_op jit(solution)/shard_map/scatter | solution.py:90
  6.6 1.1 fusion.20
  7.8 0.1 broadcast_in_dim.135
  7.9 2.4 %scatter_custom_fusion = s32[640]{0:T(1024)S(1)} fusion(s32[512]{0:T(512)S(1)} %bitcast.128, s32[512]{0:T(512)S(1)} %broadcast.429, s32[]{:T(128)} %constant.153.clone.1), kind=kCustom, calls=%fused_computation.96 | custom fusion | bytes 2564 | tf_op jit(solution)/shard_map/scatter | solution.py:91
  10.4 0.1 broadcast_in_dim.133
  10.4 1.1 fusion.22
  11.5 4.1 %gather_fusion.3 = bf16[640,2048]{1,0:T(8,128)(2,1)} fusion(bf16[64,2048]{1,0:T(8,128)(2,1)S(1)} %fusion.22, s32[1024]{0:T(1024)S(1)} %pad_clamp_fusion.1), kind=kCustom, calls=%fused_computation.3 | custom fusion | bytes 5245440 | tf_op jit(solution)/shard_map/jit(_take)/gather | solution.py:109
  15.6 3.6 %select_select_fusion = bf16[16,40,2048]{2,1,0:T(8,128)(2,1)} fusion(bf16[16,40,2048]{2,1,0:T(8,128)(2,1)} %bitcast.121, pred[16,40]{1,0:T(8,128)(4,1)S(1)} %broadcast_in_dim.135, pred[16,40]{1,0:T(8,128)(4,1)S(1)} %broadcast_in_dim.133), kind=kLoop, calls=%fused_computation.12 | loop fusion | flops 2621440 | bytes 5244160 | tf_op jit(solution)/shard_map/jit(_where)/select_n | solution.py:109
  19.3 6.7 %all-to-all-start.1 = ((bf16[16,40,2048]{2,1,0:T(8,128)(2,1)}), bf16[16,40,2048]{2,1,0:T(8,128)(2,1)}, u32[]{:S(2)}, u32[]{:S(2)}) async-start(bf16[16,40,2048]{2,1,0:T(8,128)(2,1)} %select_select_fusion), calls=%async_computation.1 | async-start | bytes 5242880 | tf_op jit(solution)/shard_map/all_to_all | solution.py:111
  26.0 3.3 %gather_fusion = bf16[16,128,512]{2,1,0:T(8,128)(2,1)} fusion(bf16[8,128,512]{2,1,0:T(8,128)(2,1)} %param.13, s32[1024]{0:T(1024)S(1)} %pad_clamp_fusion.4), kind=kCustom, calls=%fused_computation | custom fusion | bytes 4194368 | tf_op jit(solution)/shard_map/jit(_take)/gather | solution.py:70
  29.3 3.2 %select_select_fusion.1 = bf16[16,128,512]{2,1,0:T(8,128)(2,1)} fusion(bf16[16,128,512]{2,1,0:T(8,128)(2,1)} %gather_fusion, pred[16]{0:T(512)(128)(4,1)S(1)} %compare_and_fusion.2, pred[16]{0:T(512)(128)(4,1)S(1)} %get-tuple-element.8), kind=kLoop, calls=%fused_computation.14 | loop fusion | flops 2097152 | bytes 4194336 | tf_op jit(solution)/shard_map/jit(_where)/select_n | solution.py:70
  32.5 52.2 %all-to-all-done.1 = bf16[16,40,2048]{2,1,0:T(8,128)(2,1)} async-done(((bf16[16,40,2048]{2,1,0:T(8,128)(2,1)}), bf16[16,40,2048]{2,1,0:T(8,128)(2,1)}, u32[]{:S(2)}, u32[]{:S(2)}) %all-to-all-start.1) | async-done | bytes 2621472 | tf_op jit(solution)/shard_map/all_to_all | solution.py:111
  84.7 4.8 %all-to-all-start = ((bf16[16,128,512]{2,1,0:T(8,128)(2,1)}), bf16[16,128,512]{2,1,0:T(8,128)(2,1)}, u32[]{:S(2)}, u32[]{:S(2)}) async-start(bf16[16,128,512]{2,1,0:T(8,128)(2,1)} %select_select_fusion.1), calls=%async_computation | async-start | bytes 4194304 | tf_op jit(solution)/shard_map/all_to_all | solution.py:71
  89.5 7.1 %fusion = f32[640,1536]{1,0:T(8,128)S(1)} fusion(bf16[640,2048]{1,0:T(8,128)(2,1)} %bitcast.27, bf16[1,2048,1536]{2,1,0:T(8,128)(2,1)} %param.18), kind=kOutput, calls=%fused_computation.7 | convolution fusion | flops 4026531840 | bytes 12845056 | tf_op jit(solution)/shard_map/dot_general | solution.py:96
  96.6 3.8 %convolution_convert_fusion = bf16[640,2048]{1,0:T(8,128)(2,1)} fusion(bf16[1,768,2048]{2,1,0:T(8,128)(2,1)S(1)} %copy-done, f32[640,1536]{1,0:T(8,128)S(1)} %fusion), kind=kOutput, calls=%fused_computation.10 | convolution fusion | flops 2017525760 | bytes 9699328 | tf_op jit(solution)/shard_map/dot_general | solution.py:101
  100.4 36.6 %all-to-all-done = bf16[16,128,512]{2,1,0:T(8,128)(2,1)} async-done(((bf16[16,128,512]{2,1,0:T(8,128)(2,1)}), bf16[16,128,512]{2,1,0:T(8,128)(2,1)}, u32[]{:S(2)}, u32[]{:S(2)}) %all-to-all-start) | async-done | bytes 2097184 | tf_op jit(solution)/shard_map/all_to_all | solution.py:71
  137.0 4.9 %all-to-all-start.2 = ((bf16[16,40,2048]{2,1,0:T(8,128)(2,1)}), bf16[16,40,2048]{2,1,0:T(8,128)(2,1)}, u32[]{:S(2)}, u32[]{:S(2)}) async-start(bf16[16,40,2048]{2,1,0:T(8,128)(2,1)} %bitcast.122), calls=%async_computation.2 | async-start | bytes 5242880 | tf_op jit(solution)/shard_map/all_to_all | solution.py:114
  141.9 0.1 reduce_sum.65
  142.0 0.2 dynamic-slice_reduce_fusion
  142.2 2.0 copy.33
  144.3 0.1 copy.44
  144.4 0.7 copy.46
  145.1 0.6 gather_fusion.2
  145.8 0.1 compare_bitcast_fusion
  146.0 0.6 broadcast_bitcast_fusion
  146.6 0.7 pad_add_fusion
  147.3 2.2 %gather_fusion.1 = bf16[2,128,512]{2,1,0:T(8,128)(2,1)S(1)} fusion(bf16[16,128,512]{2,1,0:T(8,128)(2,1)} %all-to-all-done, s32[1024]{0:T(1024)S(1)} %pad_clamp_fusion.3), kind=kCustom, calls=%fused_computation.1 | custom fusion | bytes 524296 | tf_op jit(solution)/shard_map/jit(_take)/gather | solution.py:72
  149.5 0.8 bitcast_select_fusion.3
  150.3 1.3 fusion.61
  151.6 0.2 fusion.4
  151.9 0.4 fusion.60
  152.3 0.2 fusion.6
  152.5 0.4 fusion.13
  152.9 0.4 fusion.12
  153.3 0.9 pad_maximum_fusion
  154.2 2.0 copy.47
  156.2 44.4 %all-to-all-done.2 = bf16[16,40,2048]{2,1,0:T(8,128)(2,1)} async-done(((bf16[16,40,2048]{2,1,0:T(8,128)(2,1)}), bf16[16,40,2048]{2,1,0:T(8,128)(2,1)}, u32[]{:S(2)}, u32[]{:S(2)}) %all-to-all-start.2) | async-done | bytes 2621472 | tf_op jit(solution)/shard_map/all_to_all | solution.py:114
  200.7 7.3 %gather_fusion.4 = bf16[512,2048]{1,0:T(8,128)(2,1)} fusion(bf16[640,2048]{1,0:T(8,128)(2,1)} %bitcast.31, s32[1024]{0:T(1024)S(1)} %pad_clamp_fusion), kind=kCustom, calls=%fused_computation.4 | custom fusion | bytes 4196352 | tf_op jit(solution)/shard_map/jit(_take)/gather | solution.py:121
  208.0 4.5 %multiply_reduce_fusion = bf16[64,2048]{1,0:T(8,128)(2,1)} fusion(bf16[512,2048]{1,0:T(8,128)(2,1)} %gather_fusion.4, f32[64,8]{1,0:T(8,128)S(1)} %copy-done.5, pred[64,8]{1,0:T(8,128)(4,1)S(1)} %copy.44), kind=kLoop, calls=%fused_computation.9 | loop fusion | flops 4063232 | bytes 2361856 | tf_op jit(solution)/shard_map/reduce_sum | solution.py:125
  (44 shorter events, 0.4 us)
Async XLA Ops:
  0.6 96.0 %copy-start = (bf16[1,768,2048]{2,1,0:T(8,128)(2,1)S(1)}, bf16[1,768,2048]{2,1,0:T(8,128)(2,1)}, u32[]{:S(2)}) copy-start(bf16[1,768,2048]{2,1,0:T(8,128)(2,1)} %param.19) | copy-start | bytes 9437188
  19.3 6.7 %copy-start.7 = (s32[16,2]{0,1:T(2,128)S(1)}, s32[16,2]{0,1:T(2,128)}, u32[]{:S(2)}) copy-start(s32[16,2]{0,1:T(2,128)} %param.14) | copy-start | bytes 388
  19.3 65.4 %all-to-all-start.1 = ((bf16[16,40,2048]{2,1,0:T(8,128)(2,1)}), bf16[16,40,2048]{2,1,0:T(8,128)(2,1)}, u32[]{:S(2)}, u32[]{:S(2)}) async-start(bf16[16,40,2048]{2,1,0:T(8,128)(2,1)} %select_select_fusion), calls=%async_computation.1 | async-start | bytes 5242880 | tf_op jit(solution)/shard_map/all_to_all | solution.py:111
  84.7 52.3 %all-to-all-start = ((bf16[16,128,512]{2,1,0:T(8,128)(2,1)}), bf16[16,128,512]{2,1,0:T(8,128)(2,1)}, u32[]{:S(2)}, u32[]{:S(2)}) async-start(bf16[16,128,512]{2,1,0:T(8,128)(2,1)} %select_select_fusion.1), calls=%async_computation | async-start | bytes 4194304 | tf_op jit(solution)/shard_map/all_to_all | solution.py:71
  137.0 7.3 %copy-start.6 = (s32[64,8]{0,1:T(8,128)S(1)}, s32[64,8]{0,1:T(8,128)}, u32[]{:S(2)}) copy-start(s32[64,8]{0,1:T(8,128)} %param.20) | copy-start | bytes 6148
  137.0 7.4 %copy-start.8 = (f32[64,8]{0,1:T(8,128)S(1)}, f32[64,8]{0,1:T(8,128)}, u32[]{:S(2)}) copy-start(f32[64,8]{0,1:T(8,128)} %param.21) | copy-start | bytes 6148
  137.0 8.1 %copy-start.1 = (s32[2]{0:T(128)S(1)}, s32[2]{0:T(128)}, u32[]{:S(2)}) copy-start(s32[2]{0:T(128)} %param.15) | copy-start | bytes 28
  137.0 63.7 %all-to-all-start.2 = ((bf16[16,40,2048]{2,1,0:T(8,128)(2,1)}), bf16[16,40,2048]{2,1,0:T(8,128)(2,1)}, u32[]{:S(2)}, u32[]{:S(2)}) async-start(bf16[16,40,2048]{2,1,0:T(8,128)(2,1)} %bitcast.122), calls=%async_computation.2 | async-start | bytes 5242880 | tf_op jit(solution)/shard_map/all_to_all | solution.py:114
  141.9 8.4 %copy-start.3 = (bf16[128,512]{1,0:T(8,128)(2,1)S(1)}, bf16[128,512]{1,0:T(8,128)(2,1)}, u32[]{:S(2)}) copy-start(bf16[128,512]{1,0:T(8,128)(2,1)} %param.12) | copy-start | bytes 393220
  149.5 2.4 %copy-start.2 = (bf16[128,2048]{0,1:T(8,128)(2,1)S(1)}, bf16[128,2048]{0,1:T(8,128)(2,1)}, u32[]{:S(2)}) copy-start(bf16[128,2048]{0,1:T(8,128)(2,1)} %copy.33) | copy-start | bytes 1572868
  149.5 2.4 %copy-start.4 = (pred[128,384]{0,1:T(8,128)(4,1)S(1)}, pred[128,384]{0,1:T(8,128)(4,1)}, u32[]{:S(2)}) copy-start(pred[128,384]{0,1:T(8,128)(4,1)} %pad_add_fusion) | copy-start | bytes 147460
  200.7 7.3 %copy-start.5 = (f32[64,8]{1,0:T(8,128)S(1)}, f32[64,8]{1,0:T(8,128)}, u32[]{:S(2)}) copy-start(f32[64,8]{1,0:T(8,128)} %copy.46) | copy-start | bytes 6148
where the time goes:
time: 213 us
  waiting for transfers between devices  133 us (62%)
  local copies, waits for them, and re-layouts  29.9 us (14%)
  other arithmetic  18.7 us (9%)
  starting transfers between devices  16.3 us (8%)
  matrix products  13.4 us (6%)
    all_to_all x1, waiting for transfers between devices, expert_layer(): lax.all_to_all(outgoing, 'ctx', split_axis=0, concat_axis=0, tiled=True)  52.2 us
    all_to_all x1, waiting for transfers between devices, expert_layer(): lax.all_to_all(produced.reshape(experts, amount, produced.shape[1]), 'ctx...  44.4 us
    all_to_all x1, waiting for transfers between devices, attention_layer(): lax.all_to_all(outgoing, 'ctx', split_axis=0, concat_axis=0, tiled=True)  36.6 us
    gather x1, local copies, waits for them, and re-layouts, expert_layer(): jnp.take(returned.reshape(experts * capacity, returned.shape[2]), placeme...  7.3 us
    dot_general x1, matrix products, expert_rows(): jnp.dot(token_rows, gate_up, preferred_element_type=jnp.float32)  7.13 us
    all_to_all x1, starting transfers between devices, expert_layer(): lax.all_to_all(outgoing, 'ctx', split_axis=0, concat_axis=0, tiled=True)  6.65 us
    unnamed x22, local copies, waits for them, and re-layouts  5.73 us
    all_to_all x1, starting transfers between devices, expert_layer(): lax.all_to_all(produced.reshape(experts, amount, produced.shape[1]), 'ctx...  4.91 us
  transfers between devices with their start and end apart: 3, of which 3 were waited for; matrix products, arithmetic and copies ran while one was open for 15% of the time, Pallas kernels for 0%

commit v1 on v0

--- a/solution.py
+++ b/solution.py
@@ -65,11 +65,22 @@
     chosen_blocks = lax.dynamic_index_in_dim(selection, device_index, 0, keepdims=False)
     causal = jnp.arange(tokens)[:, None] >= jnp.arange(tokens)[None, :]
     wanted = selection // stored == device_index
+    if lax.axis_size("ctx") <= 2 * TOPK:
+        outgoing = jnp.where(
+            wanted[:, :, None, None], jnp.take(kv_cache, selection % stored, axis=0), 0
+        )
+        blocks = lax.psum_scatter(outgoing, "ctx", scatter_dimension=0, tiled=True)[0]
+        return attend(queried, blocks, fresh_kv, chosen_blocks, ctx_lengths, causal)
     local_index = jnp.sum(jnp.where(wanted, selection % stored, 0), axis=1)
     asked = jnp.any(wanted, axis=1)
     outgoing = jnp.where(asked[:, None, None], jnp.take(kv_cache, local_index, axis=0), 0)
     arrived = lax.all_to_all(outgoing, "ctx", split_axis=0, concat_axis=0, tiled=True)
     blocks = jnp.take(arrived, chosen_blocks // stored, axis=0)
+    return attend(queried, blocks, fresh_kv, chosen_blocks, ctx_lengths, causal)
+
+
+def attend(queried, blocks, fresh_kv, chosen_blocks, ctx_lengths, causal):
+    tokens = queried.shape[0]
     kv_rows = jnp.concatenate([blocks.reshape(-1, blocks.shape[2]), fresh_kv], axis=0)
     usable = key_usable(chosen_blocks, ctx_lengths)
     usable_mask = jnp.concatenate(
@@ -101,10 +112,24 @@
     return jnp.dot(active, down_proj, preferred_element_type=jnp.float32).astype(jnp.bfloat16)
 
 
+def dense_experts(normed, gate_up, down_proj, expert_ids, gate_weights):
+    experts = lax.axis_size("ctx")
+    columns = jnp.arange(experts, dtype=jnp.int32)
+    named = expert_ids[:, :, None] == columns[None, None, :]
+    gates = jnp.sum(jnp.where(named, gate_weights[:, :, None], 0.0), axis=1)
+    gates = lax.all_to_all(gates.T.reshape(experts, -1), "ctx", 0, 0, tiled=True).reshape(-1)
+    rows = lax.all_gather(normed, "ctx", axis=0, tiled=True)
+    produced = expert_rows(rows, gate_up, down_proj).astype(jnp.float32)
+    scaled = jnp.where(gates[:, None] > 0, produced * gates[:, None], 0.0).astype(jnp.bfloat16)
+    return lax.psum_scatter(scaled, "ctx", scatter_dimension=0, tiled=True)
+
+
 def expert_layer(residual_rows, norm_gain, w_gate_up, w_down, expert_ids, gate_weights):
     experts = lax.axis_size("ctx")
     capacity = max(3, 5 * expert_ids.shape[0] * TOPK // (4 * experts))
     normed = rms_normed(residual_rows, norm_gain)
+    if experts <= 2 * TOPK:
+        return dense_experts(normed, w_gate_up[0], w_down[0], expert_ids, gate_weights)
     placement, token_table, filled = slot_places(expert_ids, experts, capacity)
     outgoing = jnp.where(filled[:, None] > 0, jnp.take(normed, token_table, axis=0), 0)
     outgoing = outgoing.reshape(experts, capacity, normed.shape[1])

time: 213 us -> 222 us (1.042)
  the two profiles are of different devices: /device:TPU:11 before, /device:TPU:0 now
where the time goes in v1:
time: 222 us
  waiting for transfers between devices  155 us (70%)
  matrix products  17.9 us (8%)
  between operations  13.9 us (6%)
  blocking collectives  13.6 us (6%)
  local copies, waits for them, and re-layouts  11.2 us (5%)
  other arithmetic  10.7 us (5%)
    reduce_scatter x1, waiting for transfers between devices, dense_experts(): return lax.psum_scatter(scaled, 'ctx', scatter_dimension=0, tiled=True)  70.3 us
    reduce_scatter x1, waiting for transfers between devices, attention_layer(): lax.psum_scatter(outgoing, 'ctx', scatter_dimension=0, tiled=True)[0]  56.1 us
    all_gather x1, waiting for transfers between devices, dense_experts(): rows = lax.all_gather(normed, 'ctx', axis=0, tiled=True)  28.2 us
    all_to_all x1, blocking collectives, dense_experts(): lax.all_to_all(gates.T.reshape(experts, -1), 'ctx', 0, 0, tiled=True)  13.6 us
    dot_general x1, matrix products, expert_rows(): jnp.dot(token_rows, gate_up, preferred_element_type=jnp.float32)  10 us
    unnamed x18, local copies, waits for them, and re-layouts  5.41 us
    dot_general x1, matrix products, expert_rows(): jnp.dot(active, down_proj, preferred_element_type=jnp.float32)  5.25 us
    select_n x1, other arithmetic, attention_layer(): jnp.where(wanted[:, :, None, None], jnp.take(kv_cache, selection % stored...  4.69 us
  transfers between devices with their start and end apart: 3, of which 3 were waited for; matrix products, arithmetic and copies ran while one was open for 16% of the time, Pallas kernels for 0%

profile of v1, /device:TPU:0, one launch (start us, length us, event | category | flops | bytes accessed | tf_op | source)
XLA Modules:
  0.0 221.9 jit_solution(12986650301812330327)
XLA Ops:
  7.2 0.0 copy-start
  7.2 0.0 all-gather.2.cloned.1.call-start
  7.2 1.3 fusion.20
  8.5 1.8 fusion.22
  10.3 0.0 all-gather.2.cloned.1.call-update
  10.3 0.0 reduce-scatter.3.cloned.1.call-start
  10.4 0.7 compare_and_fusion
  11.1 0.1 copy.51
  11.1 0.1 reshape.178
  11.2 0.1 copy.49
  11.3 0.1 copy.50
  11.4 4.0 %gather_fusion = bf16[32,128,512]{2,1,0:T(8,128)(2,1)} fusion(bf16[8,128,512]{2,1,0:T(8,128)(2,1)} %param.13, s32[1024]{0:T(1024)S(1)} %pad_clamp_fusion.1), kind=kCustom, calls=%fused_computation | custom fusion | bytes 8388736 | tf_op jit(solution)/shard_map/jit(_take)/gather | solution.py:70
  15.5 4.7 %select_select_fusion = bf16[16,2,128,512]{3,2,1,0:T(8,128)(2,1)} fusion(bf16[16,2,128,512]{3,2,1,0:T(8,128)(2,1)} %bitcast.76, pred[16,2]{1,0:T(8,128)(4,1)S(1)} %copy.50, pred[16,2]{1,0:T(8,128)(4,1)S(1)} %copy.49), kind=kLoop, calls=%fused_computation.5 | loop fusion | flops 4194304 | bytes 8388672 | tf_op jit(solution)/shard_map/jit(_where)/select_n | solution.py:69
  20.1 0.0 copy-start.6
  20.1 0.0 copy-start.7
  20.2 0.0 reduce-scatter.3.cloned.1.call-update
  20.2 0.0 reduce-scatter.5.cloned.1.call-start
  20.2 0.6 copy-done.6
  20.8 0.0 copy-done.7
  20.9 13.6 %all_to_all.9 = f32[16,1,64]{2,1,0:T(1,128)S(1)} all-to-all(f32[16,1,64]{2,1,0:T(1,128)S(1)} %bitcast.84), channel_id=1, replica_groups=mesh['group'=2,'ctx'=16] {'ctx'}, dimensions={0} | all-to-all | bytes 8192 | tf_op jit(solution)/shard_map/all_to_all | solution.py:120
  34.5 0.5 broadcast.269
  35.0 0.7 reduce.6
  35.7 0.1 broadcast_in_dim_reshape.2
  35.8 28.2 %all-gather.2.cloned.1.call-done = bf16[1024,2048]{1,0:T(8,128)(2,1)} async-done(((bf16[64,2048]{1,0:T(8,128)(2,1)}), bf16[1024,2048]{1,0:T(8,128)(2,1)}) %all-gather.2.cloned.1.call-update) | async-done | bytes 4194320 | tf_op jit(solution)/shard_map/all_gather | solution.py:121
  63.9 10.0 %fusion = f32[1024,1536]{1,0:T(8,128)S(1)} fusion(bf16[1024,2048]{1,0:T(8,128)(2,1)} %all-gather.2.cloned.1.call-done, bf16[1,2048,1536]{2,1,0:T(8,128)(2,1)} %param.18), kind=kOutput, calls=%fused_computation.3 | convolution fusion | flops 6442450944 | bytes 16777216 | tf_op jit(solution)/shard_map/dot_general | solution.py:107
  73.9 0.0 copy-done
  74.0 5.3 %select_convert_fusion = bf16[1024,2048]{1,0:T(8,128)(2,1)} fusion(f32[1024]{0:T(1024)S(1)} %broadcast_in_dim_reshape.2, pred[1024]{0:T(1024)(128)(4,1)S(1)} %broadcast_compare_fusion, bf16[1,768,2048]{2,1,0:T(8,128)(2,1)S(1)} %copy-done, f32[1024,1536]{1,0:T(8,128)S(1)} %fusion), kind=kOutput, calls=%fused_computation.2 | convolution fusion | flops 3236429824 | bytes 13636608 | tf_op jit(solution)/shard_map/dot_general | solution.py:112
  79.2 0.0 reduce-scatter.5.cloned.1.call-update
  79.2 0.7 copy-done.5
  79.9 0.2 dynamic-slice_reduce_fusion
  80.1 2.1 copy.52
  82.2 0.0 copy-done.1
  82.2 0.6 gather_fusion.1
  82.8 0.1 compare_bitcast_fusion
  82.9 0.1 pad_add_fusion
  83.0 56.1 %reduce-scatter.3.cloned.1.call-done = bf16[1,2,128,512]{3,2,1,0:T(8,128)(2,1)} async-done(((bf16[16,2,128,512]{3,2,1,0:T(8,128)(2,1)}), bf16[1,2,128,512]{3,2,1,0:T(8,128)(2,1)}) %reduce-scatter.3.cloned.1.call-update) | async-done | bytes 262160 | tf_op jit(solution)/shard_map/reduce_scatter | solution.py:72
  139.1 0.0 copy-done.4
  139.1 1.4 fusion.45
  140.6 0.2 fusion.6
  140.8 0.0 copy-done.2
  140.8 0.0 copy-done.3
  140.8 0.4 fusion.44
  141.2 0.2 fusion.8
  141.4 0.4 fusion.15
  141.8 0.4 fusion.14
  142.3 0.8 pad_maximum_fusion
  143.1 2.0 copy.60
  145.1 70.3 %reduce-scatter.5.cloned.1.call-done = bf16[64,2048]{1,0:T(8,128)(2,1)} async-done(((bf16[1024,2048]{1,0:T(8,128)(2,1)}), bf16[64,2048]{1,0:T(8,128)(2,1)}) %reduce-scatter.5.cloned.1.call-update) | async-done | bytes 262160 | tf_op jit(solution)/shard_map/reduce_scatter | solution.py:124
  (14 shorter events, 0.1 us)
Async XLA Ops:
  7.2 66.8 %copy-start = (bf16[1,768,2048]{2,1,0:T(8,128)(2,1)S(1)}, bf16[1,768,2048]{2,1,0:T(8,128)(2,1)}, u32[]{:S(2)}) copy-start(bf16[1,768,2048]{2,1,0:T(8,128)(2,1)} %param.19) | copy-start | bytes 9437188
  7.2 56.8 %all-gather.2.cloned.1.call-start = ((), (), s32[]{:S(2)}) async-start(), calls=%async_computation.4 | async-start | bytes 4456448 | tf_op jit(solution)/shard_map/all_gather | solution.py:121
  10.3 128.8 %reduce-scatter.3.cloned.1.call-start = ((), (), s32[]{:S(2)}) async-start(), calls=%async_computation.3 | async-start | bytes 4456448 | tf_op jit(solution)/shard_map/reduce_scatter | solution.py:72
  20.1 0.7 copy-start.6
  20.1 0.7 copy-start.7
  20.2 195.2 %reduce-scatter.5.cloned.1.call-start = ((), (), s32[]{:S(2)}) async-start(), calls=%async_computation.5 | async-start | bytes 4456448 | tf_op jit(solution)/shard_map/reduce_scatter | solution.py:124
  79.2 0.7 copy-start.5
  79.2 2.9 %copy-start.1 = (s32[2]{0:T(128)S(1)}, s32[2]{0:T(128)}, u32[]{:S(2)}) copy-start(s32[2]{0:T(128)} %param.15) | copy-start | bytes 28
  79.2 59.9 %copy-start.4 = (bf16[128,512]{1,0:T(8,128)(2,1)S(1)}, bf16[128,512]{1,0:T(8,128)(2,1)}, u32[]{:S(2)}) copy-start(bf16[128,512]{1,0:T(8,128)(2,1)} %param.12) | copy-start | bytes 393220
  139.1 1.7 copy-start.2
  139.1 1.7 copy-start.3
Sparse Core Ops, SparseCore 0:
  10.7 53.1 all-gather.1
  67.8 71.2 reduce-scatter.2
  143.5 71.8 reduce-scatter.4

commit v2 on v0

--- a/solution.py
+++ b/solution.py
@@ -1,6 +1,10 @@
+import functools
+
 import jax
 import jax.numpy as jnp
 from jax import lax
+from jax.experimental import pallas as pl
+from jax.experimental.pallas import tpu as pltpu
 from jax.sharding import PartitionSpec as P
 
 HEADS = 16
@@ -70,6 +74,11 @@
     outgoing = jnp.where(asked[:, None, None], jnp.take(kv_cache, local_index, axis=0), 0)
     arrived = lax.all_to_all(outgoing, "ctx", split_axis=0, concat_axis=0, tiled=True)
     blocks = jnp.take(arrived, chosen_blocks // stored, axis=0)
+    return attend(queried, blocks, fresh_kv, chosen_blocks, ctx_lengths, causal)
+
+
+def attend(queried, blocks, fresh_kv, chosen_blocks, ctx_lengths, causal):
+    tokens = queried.shape[0]
     kv_rows = jnp.concatenate([blocks.reshape(-1, blocks.shape[2]), fresh_kv], axis=0)
     usable = key_usable(chosen_blocks, ctx_lengths)
     usable_mask = jnp.concatenate(
@@ -128,6 +137,280 @@
     return summed.astype(jnp.bfloat16)
 
 
+MESH = pl.DeviceIdType.MESH
+
+
+class Ring:
+    def __init__(self, count):
+        self.chips = count // 2
+        self.rows = self.chips // 2
+        me = lax.axis_index("ctx")
+        self.core = me % 2
+        chip = me // 2
+        level, column = chip // 2, chip % 2
+        self.place = level + column * (self.chips - 1 - 2 * level)
+        self.near = self.half()
+        self.used = 0
+
+    def half(self):
+        far = self.chips // 2
+        return ((far, self.chips - 1 - far), (self.chips - 1 - far, far))
+
+    def device(self, offset, core):
+        place = (self.place + offset + self.chips) % self.chips
+        column = place // self.rows
+        level = place + column * (self.chips - 1 - 2 * place)
+        return (level * 2 + column) * 2 + core
+
+    def copy(self, source, target, sems, device):
+        send, recv = sems
+        index = self.used
+        self.used += 1
+        return pltpu.make_async_remote_copy(
+            src_ref=source,
+            dst_ref=target,
+            send_sem=send.at[index],
+            recv_sem=recv.at[index],
+            device_id={"ctx": device},
+            device_id_type=MESH,
+        )
+
+    def greet(self):
+        barrier = pltpu.get_barrier_semaphore()
+        for device in self.partners():
+            pl.semaphore_signal(barrier, inc=1, device_id={"ctx": device}, device_id_type=MESH)
+        pl.semaphore_wait(barrier, 3)
+
+    def partners(self):
+        return (
+            self.device(0, 1 - self.core),
+            self.device(1, self.core),
+            self.device(-1, self.core),
+        )
+
+
+class Gather:
+    def __init__(self, ring, sems, source, target, pieces):
+        self.ring, self.sems, self.source, self.target = ring, sems, source, target
+        self.pieces = pieces
+        self.ways = {}
+        self.aside = []
+
+    def across(self, view, index):
+        ring = self.ring
+        copy = ring.copy(
+            view, self.target.at[index], self.sems, ring.device(0, 1 - ring.core)
+        )
+        copy.start()
+        self.aside.append(copy)
+
+    def step(self, number):
+        ring = self.ring
+        for at, (start, rows, lengths) in enumerate(self.pieces):
+            for side, length in zip((1, -1), lengths):
+                key = (at, side)
+                span = pl.ds(start, rows)
+                origin = ring.device(-side * number, ring.core)
+                if 0 < number <= length:
+                    self.ways[key][-1].wait_recv()
+                if number < length:
+                    view = self.source.at[span] if number == 0 else self.target.at[origin, span]
+                    copy = ring.copy(
+                        view, self.target.at[origin, span], self.sems, ring.device(side, ring.core)
+                    )
+                    copy.start()
+                    self.ways.setdefault(key, []).append(copy)
+                if 0 < number <= length:
+                    self.across(self.target.at[origin, span], (origin, span))
+        if number == 0:
+            me = ring.device(0, ring.core)
+            self.across(self.source, me)
+            self.target[me] = self.source[...]
+
+    def finish(self):
+        for copy in self.aside:
+            copy.wait()
+        for copies in self.ways.values():
+            for copy in copies:
+                copy.wait_send()
+
+
+class Scatter:
+    def __init__(self, ring, sems, source, target, other, sent, got):
+        self.ring, self.sems, self.source, self.target = ring, sems, source, target
+        self.other, self.sent, self.got = other, sent, got
+        self.rows = source.shape[1] // 2
+        self.ways, self.used = {}, 0
+        self.aside = {}
+
+    def begin(self):
+        ring = self.ring
+        far = ring.chips // 2
+        order = [far]
+        for near in range(far - 1, 0, -1):
+            order += [near, ring.chips - near]
+        order.append(0)
+        for offset in order:
+            copy = ring.copy(
+                self.source.at[ring.device(offset, 1 - ring.core)],
+                self.other.at[offset],
+                self.sems,
+                ring.device(0, 1 - ring.core),
+            )
+            copy.start()
+            self.aside[offset] = [copy, False]
+
+    def local(self, offset, span):
+        offset = offset % self.ring.chips
+        copy, seen = self.aside[offset]
+        if not seen:
+            copy.wait_recv()
+            self.aside[offset][1] = True
+        own = self.source[self.ring.device(offset, self.ring.core), span]
+        return own.astype(jnp.float32) + self.other[offset, span].astype(jnp.float32)
+
+    def step(self, number):
+        ring = self.ring
+        for at, lengths in enumerate(ring.near):
+            span = pl.ds(at * self.rows, self.rows)
+            for side, length in zip((1, -1), lengths):
+                if number >= length:
+                    continue
+                value = self.local(side * (length - number), span)
+                if number > 0:
+                    before = self.ways[at, side][-1]
+                    before[0].wait_recv()
+                    value = value + self.got[before[1]].astype(jnp.float32)
+                slot = self.used
+                self.used += 1
+                self.sent[slot] = value.astype(self.sent.dtype)
+                copy = ring.copy(
+                    self.sent.at[slot], self.got.at[slot], self.sems, ring.device(side, ring.core)
+                )
+                copy.start()
+                self.ways.setdefault((at, side), []).append((copy, slot))
+
+    def finish(self):
+        for at in range(2):
+            span = pl.ds(at * self.rows, self.rows)
+            value = self.local(0, span)
+            for side in (1, -1):
+                copy, slot = self.ways[at, side][-1]
+                copy.wait_recv()
+                value = value + self.got[slot].astype(jnp.float32)
+            self.target[span] = value.astype(self.target.dtype)
+        for copy, seen in self.aside.values():
+            copy.wait_send()
+        for copies in self.ways.values():
+            for copy, slot in copies:
+                copy.wait_send()
+
+
+def scatter_scratch(count, slots):
+    chips = count // 2
+    hops = 2 * (chips - 1)
+    rows, columns = slots.shape[1:]
+    return [
+        pltpu.VMEM((chips, rows, columns), slots.dtype),
+        pltpu.VMEM((hops, rows // 2, columns), slots.dtype),
+        pltpu.VMEM((hops, rows // 2, columns), slots.dtype),
+    ], chips + hops
+
+
+def first_kernel(count, rows_ref, gates_ref, slots_ref, all_rows, all_gates, kept, *scratch):
+    other, sent, got, send, recv = scratch
+    ring = Ring(count)
+    ring.greet()
+    sems = (send, recv)
+    half = rows_ref.shape[0] // 2
+    pieces = [(at * half, half, lengths) for at, lengths in enumerate(ring.near)]
+    gates = Gather(ring, sems, gates_ref, all_gates, [(0, gates_ref.shape[0], ring.near[0])])
+    rows = Gather(ring, sems, rows_ref, all_rows, pieces)
+    slots = Scatter(ring, sems, slots_ref, kept, other, sent, got)
+    slots.begin()
+    for number in range(ring.chips // 2 + 1):
+        gates.step(number)
+        rows.step(number)
+        slots.step(number)
+    slots.finish()
+    gates.finish()
+    rows.finish()
+
+
+def first_exchange(normed, gates, slots):
+    count = lax.axis_size("ctx")
+    scratch, sems = scatter_scratch(count, slots)
+    chips = count // 2
+    sems += 2 * 2 * (chips - 1) + 1 + 2 * (chips - 1) + 1
+    vmem = pl.BlockSpec(memory_space=pltpu.VMEM)
+    return pl.pallas_call(
+        functools.partial(first_kernel, count),
+        out_shape=(
+            jax.ShapeDtypeStruct((count,) + normed.shape, normed.dtype),
+            jax.ShapeDtypeStruct((count,) + gates.shape, gates.dtype),
+            jax.ShapeDtypeStruct(slots.shape[1:], slots.dtype),
+        ),
+        in_specs=[vmem] * 3,
+        out_specs=(vmem,) * 3,
+        scratch_shapes=scratch
+        + [pltpu.SemaphoreType.DMA((sems,)), pltpu.SemaphoreType.DMA((sems,))],
+        compiler_params=pltpu.CompilerParams(collective_id=0, has_side_effects=True),
+    )(normed, gates, slots)
+
+
+def last_kernel(count, slots_ref, kept, other, sent, got, send, recv):
+    ring = Ring(count)
+    ring.greet()
+    slots = Scatter(ring, (send, recv), slots_ref, kept, other, sent, got)
+    slots.begin()
+    for number in range(ring.chips // 2):
+        slots.step(number)
+    slots.finish()
+
+
+def last_exchange(slots):
+    count = lax.axis_size("ctx")
+    scratch, sems = scatter_scratch(count, slots)
+    vmem = pl.BlockSpec(memory_space=pltpu.VMEM)
+    return pl.pallas_call(
+        functools.partial(last_kernel, count),
+        out_shape=jax.ShapeDtypeStruct(slots.shape[1:], slots.dtype),
+        in_specs=[vmem],
+        out_specs=vmem,
+        scratch_shapes=scratch
+        + [pltpu.SemaphoreType.DMA((sems,)), pltpu.SemaphoreType.DMA((sems,))],
+        compiler_params=pltpu.CompilerParams(collective_id=1, has_side_effects=True),
+    )(slots)
+
+
+def few_devices(queries, fresh_kv, kv_cache, selection, ctx_lengths, residual_rows, norm_gain,
+                w_gate_up, w_down, expert_ids, gate_weights):
+    experts = lax.axis_size("ctx")
+    me = lax.axis_index("ctx")
+    stored = kv_cache.shape[0]
+    tokens = queries.shape[0]
+    local = expert_ids.shape[0]
+    normed = rms_normed(residual_rows, norm_gain)
+    named = expert_ids[:, :, None] == jnp.arange(experts, dtype=jnp.int32)[None, None, :]
+    gates = jnp.sum(jnp.where(named, gate_weights[:, :, None], 0.0), axis=1)
+    wanted = selection // stored == me
+    slots = jnp.where(wanted[:, :, None, None], jnp.take(kv_cache, selection % stored, axis=0), 0)
+    slots = slots.reshape(experts, -1, kv_cache.shape[2])
+    rows, all_gates, blocks = first_exchange(normed, gates.reshape(-1, 128), slots)
+    all_gates = all_gates.reshape(experts * local, experts)
+    mine = jnp.arange(experts, dtype=jnp.int32)[None, :] == me
+    gate = jnp.sum(jnp.where(mine, all_gates, 0.0), axis=1)
+    produced = expert_rows(rows.reshape(experts * local, -1), w_gate_up[0], w_down[0])
+    scaled = (produced.astype(jnp.float32) * gate[:, None]).astype(jnp.bfloat16)
+    expert_out = last_exchange(scaled.reshape(experts, local, -1))
+    queried = queries.reshape(tokens, KV_HEADS, HEADS // KV_HEADS, HEAD_DIM)
+    chosen_blocks = lax.dynamic_index_in_dim(selection, me, 0, keepdims=False)
+    causal = jnp.arange(tokens)[:, None] >= jnp.arange(tokens)[None, :]
+    blocks = blocks.reshape(-1, BLOCK, blocks.shape[1])
+    attention = attend(queried, blocks, fresh_kv, chosen_blocks, ctx_lengths, causal)
+    return (attention, expert_out)
+
+
 def shards(
     queries,
     fresh_kv,
@@ -141,6 +424,12 @@
     expert_ids,
     gate_weights,
 ):
+    count = lax.axis_size("ctx")
+    if 8 <= count <= 2 * TOPK and count % 4 == 0 and expert_ids.shape[0] * count % 1024 == 0:
+        return few_devices(
+            queries, fresh_kv, kv_cache, selection, ctx_lengths, residual_rows, norm_gain,
+            w_gate_up, w_down, expert_ids, gate_weights,
+        )
     attention = attention_layer(queries, fresh_kv, kv_cache, selection, ctx_lengths)
     expert_out = expert_layer(residual_rows, norm_gain, w_gate_up, w_down, expert_ids, gate_weights)
     return (attention, expert_out)

time: 213 us -> 127 us (0.60)
  the two profiles are of different devices: /device:TPU:11 before, /device:TPU:0 now
where the time goes in v2:
time: 127 us
  Pallas kernels  81.2 us (64%)
  matrix products  18.6 us (15%)
  local copies, waits for them, and re-layouts  15.7 us (12%)
  other arithmetic  10.4 us (8%)
    pallas_call x1, Pallas kernels, first_exchange(): pl.pallas_call(functools.partial(first_kernel, count), out_shape=(jax.Sha...  50.4 us
    pallas_call x1, Pallas kernels, last_exchange(): pl.pallas_call(functools.partial(last_kernel, count), out_shape=jax.Shape...  30.8 us
    dot_general x1, matrix products, expert_rows(): jnp.dot(token_rows, gate_up, preferred_element_type=jnp.float32)  10 us
    unnamed x24, local copies, waits for them, and re-layouts  5.95 us
    select_n x1, other arithmetic, few_devices(): jnp.where(wanted[:, :, None, None], jnp.take(kv_cache, selection % stored...  5.32 us
    dot_general x1, matrix products, expert_rows(): jnp.dot(active, down_proj, preferred_element_type=jnp.float32)  5.08 us
    gather x1, local copies, waits for them, and re-layouts, few_devices(): jnp.take(kv_cache, selection % stored, axis=0)  4.01 us

profile of v2, /device:TPU:0, one launch (start us, length us, event | category | flops | bytes accessed | tf_op | source)
XLA Modules:
  0.0 126.7 jit_solution(18102060832795153713)
XLA Ops:
  0.6 0.0 copy-start
  0.6 1.0 dynamic-slice_reduce_fusion
  1.7 0.7 compare_and_fusion
  2.4 0.1 copy.39
  2.5 0.1 reshape.192
  2.6 4.0 %gather_fusion = bf16[32,128,512]{2,1,0:T(8,128)(2,1)} fusion(bf16[8,128,512]{2,1,0:T(8,128)(2,1)} %param.13, s32[1024]{0:T(1024)S(1)} %get-tuple-element.24), kind=kCustom, calls=%fused_computation | custom fusion | bytes 8388736 | tf_op jit(solution)/shard_map/jit(_take)/gather | solution.py:397
  6.6 0.1 copy.37
  6.7 0.1 broadcast_in_dim.100
  6.8 0.1 copy.38
  6.9 0.1 broadcast_in_dim.103
  7.0 0.0 copy-start.4
  7.0 0.0 copy-start.7
  7.0 0.0 copy-start.8
  7.0 0.0 copy-start.9
  7.0 5.3 %fusion.2.slots_ref = bf16[16,256,512]{2,1,0:T(8,128)(2,1)} fusion(pred[16,256]{1,0:T(8,128)(4,1)S(1)} %get-tuple-element.25, pred[16,256]{1,0:T(8,128)(4,1)S(1)} %get-tuple-element.26, bf16[16,256,512]{2,1,0:T(8,128)(2,1)} %bitcast.82), kind=kLoop, calls=%fused_computation.6 | loop fusion | flops 4194304 | bytes 8396800 | tf_op jit(solution)/shard_map/jit(_where)/select_n | solution.py:397
  12.3 0.0 copy-done.4
  12.3 0.2 fusion.21
  12.5 0.0 copy-done.7
  12.5 0.8 fusion.23.rows_ref
  13.3 0.0 copy-done.8
  13.3 0.0 copy-done.9
  13.4 0.1 copy.36
  13.5 0.7 reshape.185.gates_ref
  14.1 50.4 %shard_map.122 = (bf16[16,64,2048]{2,1,0:T(8,128)(2,1)}, f32[16,8,128]{2,1,0:T(8,128)}, bf16[256,512]{1,0:T(8,128)(2,1)}) custom-call(bf16[64,2048]{1,0:T(8,128)(2,1)} %fusion.23.rows_ref, f32[8,128]{1,0:T(8,128)} %reshape.185.gates_ref, bf16[16,256,512]{2,1,0:T(8,128)(2,1)} %fusion.2.slots_ref), custom_call_target="tpu_custom_call" | custom-call | tf_op jit(solution)/shard_map/pallas_call | solution.py:346
  64.6 1.8 %reshape.188 = f32[1024,16]{1,0:T(8,128)} reshape(f32[16,8,128]{2,1,0:T(8,128)} %get-tuple-element.7) | data formatting | bytes 131072 | tf_op jit(solution)/shard_map/reshape | solution.py:400
  66.4 1.2 select_reduce_fusion
  67.7 10.0 %fusion = f32[1024,1536]{1,0:T(8,128)S(1)} fusion(bf16[1024,2048]{1,0:T(8,128)(2,1)} %bitcast.91, bf16[1,2048,1536]{2,1,0:T(8,128)(2,1)} %param.18), kind=kOutput, calls=%fused_computation.3 | convolution fusion | flops 6442450944 | bytes 16777216 | tf_op jit(solution)/shard_map/dot_general | solution.py:105
  77.7 0.0 copy-done
  77.7 5.1 %multiply_convert_fusion = bf16[1024,2048]{1,0:T(8,128)(2,1)} fusion(f32[1024]{0:T(1024)S(1)} %select_reduce_fusion, bf16[1,768,2048]{2,1,0:T(8,128)(2,1)S(1)} %copy-done, f32[1024,1536]{1,0:T(8,128)S(1)} %fusion), kind=kOutput, calls=%fused_computation.2 | convolution fusion | flops 3234332672 | bytes 13635584 | tf_op jit(solution)/shard_map/dot_general | solution.py:110
  82.8 30.8 %shard_map.123 = bf16[64,2048]{1,0:T(8,128)(2,1)} custom-call(bf16[16,64,2048]{2,1,0:T(8,128)(2,1)} %bitcast.83), custom_call_target="tpu_custom_call" | custom-call | tf_op jit(solution)/shard_map/pallas_call | solution.py:375
  113.6 0.0 copy-done.1
  113.6 0.6 gather_fusion.1
  114.2 0.1 compare_bitcast_fusion
  114.3 0.7 pad_add_fusion
  115.1 1.0 constant_dynamic-update-slice_fusion.1
  116.0 0.9 constant_dynamic-update-slice_fusion
  117.0 0.0 copy-start.5
  117.0 2.2 %copy.40 = bf16[128,2048]{0,1:T(8,128)(2,1)} copy(bf16[128,2048]{1,0:T(8,128)(2,1)} %param.11) | data formatting | bytes 1048576 | tf_op args[0]
  119.2 1.4 %fusion.30 = (f32[8,128]{1,0:T(8,128)S(1)}, f32[8,128,384]{1,2,0:T(8,128)S(1)}) fusion(bf16[128,2,8,128]{0,3,2,1:T(8,128)(2,1)} %bitcast.84, bf16[384,512]{1,0:T(8,128)(2,1)S(1)} %constant_dynamic-update-slice_fusion, pred[128,384]{0,1:T(8,128)(4,1)} %pad_add_fusion), kind=kOutput, calls=%fused_computation.82 | convolution fusion | flops 101841920 | bytes 1986560 | tf_op jit(solution)/shard_map/tgd,ld->gtl/dot_general | solution.py:40
  120.6 0.2 fusion.7
  120.8 0.4 fusion.16
  121.2 0.4 fusion.29
  121.6 0.2 fusion.9
  121.9 1.3 %fusion.15 = bf16[128,1,8,128]{0,3,2,1:T(8,128)(2,1)S(1)} fusion(f32[8,128,384]{1,2,0:T(8,128)S(1)} %get-tuple-element.20, f32[8,128]{1,0:T(8,128)S(1)} %get-tuple-element.19, f32[128,8]{0,1:T(8,128)S(1)} %bitcast.89, bf16[384,512]{1,0:T(8,128)(2,1)} %copy-done.5), kind=kOutput, calls=%fused_computation.25 | convolution fusion | flops 101711872 | bytes 1941504 | tf_op jit(solution)/shard_map/gtl,ld->tgd/dot_general | solution.py:53
  123.2 0.8 pad_maximum_fusion
  124.0 2.0 %copy.47 = bf16[128,2048]{1,0:T(8,128)(2,1)} copy(bf16[128,2048]{0,1:T(8,128)(2,1)} %bitcast.86) | data formatting | bytes 1048576
  126.0 0.0 copy-done.3
  126.0 0.7 copy.62
  (16 shorter events, 0.1 us)
Async XLA Ops:
  0.6 77.0 %copy-start = (bf16[1,768,2048]{2,1,0:T(8,128)(2,1)S(1)}, bf16[1,768,2048]{2,1,0:T(8,128)(2,1)}, u32[]{:S(2)}) copy-start(bf16[1,768,2048]{2,1,0:T(8,128)(2,1)} %param.19) | copy-start | bytes 9437188
  7.0 5.4 %copy-start.4 = (bf16[64,2048]{1,0:T(8,128)(2,1)S(1)}, bf16[64,2048]{1,0:T(8,128)(2,1)}, u32[]{:S(2)}) copy-start(bf16[64,2048]{1,0:T(8,128)(2,1)} %param.16) | copy-start | bytes 786436
  7.0 5.5 %copy-start.7 = (f32[2048]{0:T(1024)S(1)}, f32[2048]{0:T(1024)}, u32[]{:S(2)}) copy-start(f32[2048]{0:T(1024)} %param.17) | copy-start | bytes 24580
  7.0 6.4 %copy-start.8 = (f32[64,8]{0,1:T(8,128)S(1)}, f32[64,8]{0,1:T(8,128)}, u32[]{:S(2)}) copy-start(f32[64,8]{0,1:T(8,128)} %param.21) | copy-start | bytes 6148
  7.0 6.3 %copy-start.9 = (s32[64,8]{0,1:T(8,128)S(1)}, s32[64,8]{0,1:T(8,128)}, u32[]{:S(2)}) copy-start(s32[64,8]{0,1:T(8,128)} %param.20) | copy-start | bytes 6148
  82.8 30.8 %copy-start.1 = (s32[2]{0:T(128)S(1)}, s32[2]{0:T(128)}, u32[]{:S(2)}) copy-start(s32[2]{0:T(128)} %param.15) | copy-start | bytes 28
  117.0 4.2 %copy-start.5 = (bf16[384,512]{1,0:T(8,128)(2,1)}, bf16[384,512]{1,0:T(8,128)(2,1)S(1)}, u32[]{:S(2)}) copy-start(bf16[384,512]{1,0:T(8,128)(2,1)S(1)} %constant_dynamic-update-slice_fusion) | copy-start | bytes 1179652
  119.2 2.1 %copy-start.2 = (bf16[128,2048]{0,1:T(8,128)(2,1)S(1)}, bf16[128,2048]{0,1:T(8,128)(2,1)}, u32[]{:S(2)}) copy-start(bf16[128,2048]{0,1:T(8,128)(2,1)} %copy.40) | copy-start | bytes 1572868
  119.2 2.1 %copy-start.6 = (pred[128,384]{0,1:T(8,128)(4,1)S(1)}, pred[128,384]{0,1:T(8,128)(4,1)}, u32[]{:S(2)}) copy-start(pred[128,384]{0,1:T(8,128)(4,1)} %pad_add_fusion) | copy-start | bytes 147460
  121.6 4.4 %copy-start.3 = (bf16[64,2048]{1,0:T(8,128)(2,1)S(1)}, bf16[64,2048]{1,0:T(8,128)(2,1)}, u32[]{:S(2)}) copy-start(bf16[64,2048]{1,0:T(8,128)(2,1)} %shard_map.123) | copy-start | bytes 786436
